TPU v7x, 768 devices: a whole 4x8x12 slice. The times are simulated.
768 devices in a mesh: cd: 48 (over x_lo, z, core), ij: 16 (over y, x_hi).
Axes of the slice: x: 4 (x_hi: 2, x_lo: 2; x = x_hi * 2 + x_lo), y: 8, z: 12, core: 2. Of those that a mesh axis runs over, the one named last changes fastest.
Arguments:
- left_factor: bfloat16 [24576, 4096], P('cd'), may hold values from -6 to 6
- right_factor: bfloat16 [4096, 4, 1024], P(None, None, 'ij'), may hold values from -0.09375 to 0.09375
- amplitudes: float32 [192, 1152, 1024], P('ij', 'cd'), may hold values from -0.015625 to 0.015625
- heights: int32 [48], P('cd'), may hold values from 256 to 512, as said below
- owner_map: int32 [48, 512, 1], P('cd'), may hold values from 0 to 47; in each aligned block of 512 rows (0 to 511, 512 to 1023, ..., all dimensions but the last counted through in order) at most 16 rows name the same one
- row_site: int32 [48, 512], P('cd'), may hold values from 0 to 23
Outputs:
- residual: float32 [768], P(('ij', 'cd'))
Inputs may be any that keep to these rules, and one draw needn't show every extreme that they name: `heights`: some former has exactly 512 live rows. `owner_map`: within the 512 rows of one former no tile is named more than 16 times, and that bound is reached.
All inputs are finite; a program needn't handle non-finite values.
Results may differ from a plain program's by a relative error of at most 0.0028.
Values may be sent and summed in bfloat16 or wider, within the bound.
No kernel may reach another device: no remote copies, remote signals or barrier semaphores. Data moves between devices by JAX's collectives and lax.ppermute only.
A program may use at most 32 MiB of HBM per device.

v0:
```python
import jax
import jax.numpy as jnp
from jax import lax
from jax.sharding import PartitionSpec as P


def laid_out(pieces, dim):
    dims = list(pieces.shape[1:])
    dims[dim] *= pieces.shape[0]
    return jnp.moveaxis(pieces, 0, dim).reshape(dims)


def sent_to_all(array, axis):
    copies = jnp.broadcast_to(array, (lax.axis_size(axis), *array.shape))
    return lax.all_to_all(copies, axis, split_axis=0, concat_axis=0, tiled=True)


def collect(array, axis, dim):
    return laid_out(sent_to_all(array, axis), dim)


def in_blocks(array, dim, count):
    dims = array.shape
    pieces = array.reshape(*dims[:dim], count, dims[dim] // count, *dims[dim + 1 :])
    return jnp.moveaxis(pieces, dim, 0)


def summed_on_arrival(array, axis, dim):
    pieces = in_blocks(array, dim, lax.axis_size(axis))
    arrived = lax.all_to_all(pieces, axis, split_axis=0, concat_axis=0, tiled=True)
    return arrived.sum(axis=0)


def contract(amplitudes, sums):
    return jnp.einsum("icd,cbd->ib", amplitudes, sums, precision=lax.Precision.HIGHEST)


def on_device(left_factor, right_factor, amplitudes, heights, owner_map, row_site):
    rows = left_factor.shape[0]
    formers = lax.axis_size("cd")
    capacity = (rows + formers - 1) // formers + rows // (2 * formers)
    bwidth = right_factor.shape[1]
    dpiece = right_factor.shape[2]
    tile = amplitudes.shape[1]
    panel = jnp.dot(
        left_factor,
        right_factor.reshape(right_factor.shape[0], -1),
        preferred_element_type=jnp.float32,
    )
    position = jnp.arange(rows, dtype=jnp.int32)
    live = position < heights[0]
    panel = jnp.where(live[:, None], panel, 0.0).astype(jnp.bfloat16)
    owners = owner_map[0, :, 0]
    hits = (owners[:, None] == jnp.arange(formers, dtype=jnp.int32)[None, :]) & live[:, None]
    places = jnp.cumsum(hits.astype(jnp.int32), axis=0) - 1
    within = jnp.sum(jnp.where(hits, places, 0), axis=1)
    target = jnp.where(live, owners * capacity + within, -1)
    dispatch = jnp.arange(formers * capacity, dtype=jnp.int32)[:, None] == target[None, :]
    outgoing = jnp.dot(
        dispatch.astype(jnp.bfloat16), panel, preferred_element_type=jnp.float32
    ).astype(jnp.bfloat16)
    labels = jnp.dot(dispatch.astype(jnp.float32), row_site[0].astype(jnp.float32)).astype(
        jnp.int32
    )
    outgoing = outgoing.reshape(formers, capacity, bwidth, dpiece)
    labels = labels.reshape(formers, capacity)
    arrived, arrived_labels = (
        lax.all_to_all(outgoing, "cd", split_axis=0, concat_axis=0, tiled=True),
        lax.all_to_all(labels, "cd", split_axis=0, concat_axis=0, tiled=True),
    )
    arrived = arrived.reshape(formers * capacity, bwidth, dpiece)
    picker = (
        jnp.arange(tile, dtype=jnp.int32)[:, None] == arrived_labels.reshape(-1)[None, :]
    ).astype(jnp.bfloat16)
    whole = collect(
        jnp.einsum("cr,rbd->cbd", picker, arrived, preferred_element_type=jnp.float32), "ij", 2
    )
    partial_value = contract(amplitudes, whole)
    return summed_on_arrival(partial_value.reshape(-1), "cd", 0)


def solution(mesh):
    placed = (
        P("cd", None),
        P(None, None, "ij"),
        P("ij", "cd", None),
        P("cd"),
        P("cd", None, None),
        P("cd", None),
    )
    return jax.shard_map(
        on_device, mesh=mesh, in_specs=placed, out_specs=P(("ij", "cd")), check_vma=False
    )
```

profile of v0, /device:TPU:1, one launch (start us, length us, event | category | flops | bytes accessed | tf_op | source)
XLA Modules:
  0.0 115.9 jit_solution(5371231990220933825)
XLA Ops:
  0.8 0.7 fusion.18
  1.5 1.2 %reduce-window.6 = s32[48,4,128]{2,0,1:T(8,128)S(1)} reduce-window(s32[48,4,128]{2,0,1:T(8,128)S(1)} %fusion.18, s32[]{:T(128)} %constant.12.clone.1), window={size=1x1x128 pad=0_0x0_0x127_0}, to_apply=%region_0.1 | reduce-window | flops 3121152 | bytes 196612 | tf_op jit(solution)/shard_map/reduce-window
  2.7 0.2 slice_reduce_fusion
  3.0 0.8 fusion.15
  3.8 0.7 add_select_fusion
  4.5 1.1 fusion.6
  5.5 0.7 all_to_all.18
  6.2 17.9 %all-to-all-start = ((s32[48,1,16]{2,1,0:T(1,128)}), s32[48,1,16]{2,1,0:T(1,128)S(1)}, u32[]{:S(2)}, u32[]{:S(2)}) async-start(s32[48,1,16]{2,1,0:T(1,128)} %bitcast.6), calls=%async_computation | async-start | bytes 49152 | tf_op jit(solution)/shard_map/all_to_all | solution.py:69
  24.1 4.1 %fusion.4 = bf16[768,256]{1,0:T(8,128)(2,1)S(1)} fusion(bf16[512,4096]{1,0:T(8,128)(2,1)} %param.6, bf16[4096,256]{0,1:T(8,128)(2,1)S(1)} %bitcast.47, s32[512]{0:T(512)S(1)} %add_select_fusion, pred[512]{0:T(512)(128)(4,1)S(1)} %iota_compare_fusion.10), kind=kOutput, calls=%fused_computation.5 | convolution fusion | flops 1275920384 | bytes 6687232 | tf_op jit(solution)/shard_map/dot_general | solution.py:59
  28.3 0.3 reshape.67
  28.6 1.1 copy.35
  29.7 2.7 %reshape.85 = bf16[48,2,2048]{2,1,0:T(2,128)(2,1)} reshape(bf16[48,4,16,64]{3,2,1,0:T(8,128)(2,1)} %bitcast.49) | data formatting | bytes 786432
  32.3 2.2 %all-to-all-done = s32[48,1,16]{2,1,0:T(1,128)S(1)} async-done(((s32[48,1,16]{2,1,0:T(1,128)}), s32[48,1,16]{2,1,0:T(1,128)S(1)}, u32[]{:S(2)}, u32[]{:S(2)}) %all-to-all-start) | async-done | bytes 3104 | tf_op jit(solution)/shard_map/all_to_all | solution.py:69
  34.6 8.8 %all-to-all-start.1 = ((bf16[48,2,2048]{2,1,0:T(2,128)(2,1)}), bf16[48,2,2048]{2,1,0:T(2,128)(2,1)S(1)}, u32[]{:S(2)}, u32[]{:S(2)}) async-start(bf16[48,2,2048]{2,1,0:T(2,128)(2,1)} %reshape.85), calls=%async_computation.1 | async-start | bytes 786432 | tf_op jit(solution)/shard_map/all_to_all | solution.py:68
  43.4 0.5 broadcast.49
  43.9 0.7 reduce.9
  44.7 16.4 %all-to-all-done.1 = bf16[48,2,2048]{2,1,0:T(2,128)(2,1)S(1)} async-done(((bf16[48,2,2048]{2,1,0:T(2,128)(2,1)}), bf16[48,2,2048]{2,1,0:T(2,128)(2,1)S(1)}, u32[]{:S(2)}, u32[]{:S(2)}) %all-to-all-start.1) | async-done | bytes 393248 | tf_op jit(solution)/shard_map/all_to_all | solution.py:68
  61.1 0.5 reshape.86
  61.6 0.1 copy.20
  61.7 0.2 fusion.20
  62.0 0.1 broadcast_in_dim.33
  62.1 0.7 reshape.87
  62.9 24.0 %all_to_all.29 = f32[16,1,6144]{2,1,0:T(1,128)S(1)} all-to-all(f32[16,1,6144]{2,1,0:T(1,128)S(1)} %reshape.87), channel_id=1, replica_groups=mesh['cd'=48,'ij'=16] {'ij'}, dimensions={0} | all-to-all | bytes 786432 | tf_op jit(solution)/shard_map/all_to_all | solution.py:15
  86.8 0.5 broadcast.52
  87.3 1.6 %reduce.10 = f32[16,6144]{1,0:T(8,128)S(1)} reduce(f32[16,1,6144]{2,1,0:T(1,128)S(1)} %all_to_all.29, f32[]{:T(128)} %broadcast.52), dimensions={1}, to_apply=%all_to_all.21.reduce_sub_computation | reduce | bytes 786436 | tf_op jit(solution)/shard_map/all_to_all | solution.py:15
  88.9 0.5 reshape.88
  89.4 1.3 %copy.23 = f32[24,4,16,64]{3,2,1,0:T(8,128)} copy(f32[24,4,16,64]{3,1,0,2:T(4,128)S(1)} %bitcast.51) | data formatting | bytes 786432 | tf_op jit(solution)/shard_map/transpose | solution.py:10
  90.8 1.4 %reshape.69 = f32[24,4,1024]{2,1,0:T(4,128)S(1)} reshape(f32[24,4,16,64]{3,2,1,0:T(8,128)} %copy.23) | data formatting | bytes 786432 | tf_op jit(solution)/shard_map/reshape | solution.py:10
  92.2 3.6 %fusion.7 = f32[12,4]{0,1:T(4,128)S(1)} fusion(f32[24,4,1024]{2,1,0:T(4,128)S(1)} %reshape.69, f32[12,24,1024]{2,1,0:T(8,128)} %param.8), kind=kOutput, calls=%fused_computation.9 | convolution fusion | flops 14155776 | bytes 1573056 | tf_op jit(solution)/shard_map/icd,cbd->ib/dot_general | solution.py:35
  95.9 0.1 all_to_all.24
  96.0 19.2 %all_to_all.30 = f32[48,1,1]{2,1,0:T(1,128)S(1)} all-to-all(f32[48,1,1]{2,1,0:T(1,128)S(1)} %all_to_all.24), channel_id=1, replica_groups=mesh['cd'=48,'ij'=16] {'cd'}, dimensions={0} | all-to-all | bytes 384 | tf_op jit(solution)/shard_map/all_to_all | solution.py:30
  115.2 0.7 reduce_sum.21
  (10 shorter events, 0.3 us)
Async XLA Ops:
  0.0 24.1 %copy-start = (bf16[4096,4,64]{0,2,1:T(8,128)(2,1)S(1)}, bf16[4096,4,64]{0,2,1:T(8,128)(2,1)}, u32[]{:S(2)}) copy-start(bf16[4096,4,64]{0,2,1:T(8,128)(2,1)} %param.7) | copy-start | bytes 6291460
  6.2 28.3 %all-to-all-start = ((s32[48,1,16]{2,1,0:T(1,128)}), s32[48,1,16]{2,1,0:T(1,128)S(1)}, u32[]{:S(2)}, u32[]{:S(2)}) async-start(s32[48,1,16]{2,1,0:T(1,128)} %bitcast.6), calls=%async_computation | async-start | bytes 49152 | tf_op jit(solution)/shard_map/all_to_all | solution.py:69
  34.6 26.5 %all-to-all-start.1 = ((bf16[48,2,2048]{2,1,0:T(2,128)(2,1)}), bf16[48,2,2048]{2,1,0:T(2,128)(2,1)S(1)}, u32[]{:S(2)}, u32[]{:S(2)}) async-start(bf16[48,2,2048]{2,1,0:T(2,128)(2,1)} %reshape.85), calls=%async_computation.1 | async-start | bytes 786432 | tf_op jit(solution)/shard_map/all_to_all | solution.py:68
where the time goes:
time: 116 us
  blocking collectives  43.2 us (37%)
  starting transfers between devices  26.7 us (23%)
  waiting for transfers between devices  18.6 us (16%)
  local copies, waits for them, and re-layouts  11.1 us (10%)
  matrix products  8.98 us (8%)
  other arithmetic  6.35 us (5%)
    all_to_all x1, blocking collectives, sent_to_all(): return lax.all_to_all(copies, axis, split_axis=0, concat_axis=0, tiled=True)  24 us
    all_to_all x1, blocking collectives, summed_on_arrival(): lax.all_to_all(pieces, axis, split_axis=0, concat_axis=0, tiled=True)  19.2 us
    all_to_all x1, starting transfers between devices, on_device(): lax.all_to_all(labels, 'cd', split_axis=0, concat_axis=0, tiled=True)  17.9 us
    all_to_all x1, waiting for transfers between devices, on_device(): lax.all_to_all(outgoing, 'cd', split_axis=0, concat_axis=0, tiled=True)  16.4 us
    all_to_all x1, starting transfers between devices, on_device(): lax.all_to_all(outgoing, 'cd', split_axis=0, concat_axis=0, tiled=True)  8.8 us
    unnamed x6, local copies, waits for them, and re-layouts  4.42 us
    dot_general x1, matrix products, on_device(): jnp.dot(dispatch.astype(jnp.bfloat16), panel, preferred_element_type=jnp....  4.13 us
    dot_general x1, matrix products, contract(): jnp.einsum('icd,cbd->ib', amplitudes, sums, precision=lax.Precision.HIGHEST)  3.58 us
  transfers between devices with their start and end apart: 2, of which 2 were waited for; matrix products, arithmetic and copies ran while one was open for 8% of the time, Pallas kernels for 0%

commit v1 on v0

v1 whole, which is shorter than its diff:
```python
import jax
import jax.numpy as jnp
from jax import lax
from jax.experimental import pallas as pl
from jax.experimental.pallas import tpu as pltpu
from jax.sharding import PartitionSpec as P

SLOTS = 16
LANES = 128
KSTEPS = 8
QBITS = 14


def form_kernel(heights, place, owners, sites, left, right, out, acc, dispatch, tags):
    step = pl.program_id(0)
    rows = left.shape[0]
    formers = out.shape[0]
    slots = formers * SLOTS

    @pl.when(step == 0)
    def _():
        acc[...] = jnp.zeros_like(acc)
        live = lax.broadcasted_iota(jnp.int32, (1, rows), 1) < heights[0]
        owner = jnp.where(live, owners[...], -1)
        hits = lax.broadcasted_iota(jnp.int32, (formers, rows), 0) == owner
        hits_f = jnp.where(hits, 1.0, 0.0)
        upto = lax.broadcasted_iota(jnp.int32, (rows, rows), 0) <= lax.broadcasted_iota(
            jnp.int32, (rows, rows), 1
        )
        upto = jnp.where(upto, 1.0, 0.0).astype(jnp.bfloat16)
        count = jnp.dot(hits_f.astype(jnp.bfloat16), upto, preferred_element_type=jnp.float32)
        within = jnp.sum(hits_f * count, axis=0, keepdims=True).astype(jnp.int32) - 1
        target = jnp.where(live, owner * SLOTS + within, -1)
        chosen = lax.broadcasted_iota(jnp.int32, (slots, rows), 0) == target
        dispatch[...] = jnp.where(chosen, 1.0, 0.0).astype(jnp.bfloat16)
        lane = within + (place[0] % (LANES // SLOTS)) * SLOTS
        at_lane = lax.broadcasted_iota(jnp.int32, (LANES, rows), 0) == lane
        at_lane = jnp.where(at_lane, 1.0, 0.0).astype(jnp.bfloat16)
        tagged = hits_f * (sites[...] + 1).astype(jnp.float32)
        tags[...] = lax.dot_general(
            tagged.astype(jnp.bfloat16),
            at_lane,
            (((1,), (1,)), ((), ())),
            preferred_element_type=jnp.float32,
        )

    acc[...] += lax.dot_general(
        left[...], right[...], (((1,), (1,)), ((), ())), preferred_element_type=jnp.float32
    )

    @pl.when(step == KSTEPS - 1)
    def _():
        panel = acc[...].astype(jnp.bfloat16)
        moved = jnp.dot(dispatch[...], panel, preferred_element_type=jnp.float32)
        moved = moved.astype(jnp.bfloat16)
        width = moved.shape[1] // LANES
        for part in range(width):
            piece = moved[:, part * LANES : (part + 1) * LANES]
            out[:, part * SLOTS : (part + 1) * SLOTS, :] = piece.reshape(formers, SLOTS, LANES)
        tag = jnp.broadcast_to(tags[...][:, None, :], (formers, 8, LANES))
        out[:, width * SLOTS : width * SLOTS + 8, :] = tag.astype(jnp.bfloat16)


def form(heights, place, owners, sites, left, right, formers):
    rows, naux = left.shape
    cols = right.shape[0]
    block = naux // KSTEPS
    depth = cols // LANES * SLOTS + 8
    return pl.pallas_call(
        form_kernel,
        grid=(KSTEPS,),
        in_specs=[
            pl.BlockSpec(memory_space=pltpu.SMEM),
            pl.BlockSpec(memory_space=pltpu.SMEM),
            pl.BlockSpec((1, rows), lambda k: (0, 0)),
            pl.BlockSpec((1, rows), lambda k: (0, 0)),
            pl.BlockSpec((rows, block), lambda k: (0, k)),
            pl.BlockSpec((cols, block), lambda k: (0, k)),
        ],
        out_specs=pl.BlockSpec((formers, depth, LANES), lambda k: (0, 0, 0)),
        out_shape=jax.ShapeDtypeStruct((formers, depth, LANES), jnp.bfloat16),
        scratch_shapes=[
            pltpu.VMEM((rows, cols), jnp.float32),
            pltpu.VMEM((formers * SLOTS, rows), jnp.bfloat16),
            pltpu.VMEM((formers, LANES), jnp.float32),
        ],
        compiler_params=pltpu.CompilerParams(dimension_semantics=("arbitrary",)),
        name="form",
    )(heights, place, owners, sites, left, right)


def combine_kernel(arrived, out):
    formers = arrived.shape[0]
    copies, depth, cols = out.shape
    tile = depth - 8
    width = cols // LANES
    group = LANES // SLOTS
    tags = arrived[:, width * SLOTS : width * SLOTS + 8, :].astype(jnp.float32)
    site = lax.broadcasted_iota(jnp.int32, (tile, LANES), 0).astype(jnp.float32) + 1.0
    pickers = []
    for g in range(formers // group):
        tag = jnp.sum(tags[g * group : (g + 1) * group], axis=0)
        tag = jnp.concatenate([tag] * (tile // 8), axis=0)
        pickers.append(jnp.where(tag == site, 1.0, 0.0).astype(jnp.bfloat16))
    picker = jnp.concatenate(pickers, axis=1)
    for part in range(width):
        rows = arrived[:, part * SLOTS : (part + 1) * SLOTS, :].reshape(formers * SLOTS, LANES)
        sums = jnp.dot(picker, rows, preferred_element_type=jnp.float32)
        top = jnp.maximum(jnp.max(jnp.abs(sums), axis=0, keepdims=True), 2.0**-100)
        power = jnp.ceil(jnp.log(top) * 1.4426950408889634)
        coded = jnp.round(sums * jnp.exp2(QBITS - power))
        whole = jnp.concatenate([coded, jnp.broadcast_to(power, (8, LANES))], axis=0)
        whole = whole.astype(jnp.int32).astype(jnp.int16)
        for copy in range(copies):
            out[copy, :, part * LANES : (part + 1) * LANES] = whole


def combine(arrived, copies, tile, cols):
    return pl.pallas_call(
        combine_kernel,
        out_shape=jax.ShapeDtypeStruct((copies, tile + 8, cols), jnp.int16),
        name="combine",
    )(arrived)


def contract_kernel(amplitudes, pieces, out, sums, ends):
    pairs, tile, _ = amplitudes.shape
    count, _, cols = pieces.shape
    dpiece = LANES // 2
    bwidth = cols // dpiece
    low = lax.broadcasted_iota(jnp.int32, (tile, LANES), 1) < dpiece
    for two in range(count // 2):
        both = []
        for j in (2 * two, 2 * two + 1):
            whole = pieces[j].astype(jnp.int32).astype(jnp.float32)
            both.append(whole[:tile] * jnp.exp2(whole[tile : tile + 1] - QBITS))
        for half in range(cols // LANES):
            a, b = [v[:, half * LANES : (half + 1) * LANES] for v in both]
            span = slice(two * LANES, (two + 1) * LANES)
            sums[2 * half, :, span] = jnp.where(low, a, pltpu.roll(b, dpiece, 1))
            sums[2 * half + 1, :, span] = jnp.where(low, pltpu.roll(a, dpiece, 1), b)
    some = 6
    for first in range(0, pairs, some):
        totals = [[jnp.zeros((8, LANES), jnp.float32) for _ in range(bwidth)] for _ in range(some)]
        for c in range(0, tile, 8):
            for d in range(0, amplitudes.shape[2], LANES):
                s = [sums[b, c : c + 8, d : d + LANES] for b in range(bwidth)]
                for i in range(some):
                    t = amplitudes[first + i, c : c + 8, d : d + LANES]
                    for b in range(bwidth):
                        totals[i][b] = totals[i][b] + t * s[b]
        for i in range(some):
            for b in range(bwidth):
                at = (first + i) * bwidth + b
                ends[at : at + 1, :] = jnp.sum(totals[i][b], axis=0, keepdims=True)
    total = jnp.sum(ends[...], axis=1, keepdims=True)
    out[...] = jnp.broadcast_to(total, ends.shape)[:, None, :]


def contract(amplitudes, pieces):
    pairs, tile, virt = amplitudes.shape
    bwidth = pieces.shape[2] * 2 // LANES
    return pl.pallas_call(
        contract_kernel,
        out_shape=jax.ShapeDtypeStruct((pairs * bwidth, 1, LANES), jnp.float32),
        scratch_shapes=[
            pltpu.VMEM((bwidth, tile, virt), jnp.float32),
            pltpu.VMEM((pairs * bwidth, LANES), jnp.float32),
        ],
        name="contract",
    )(amplitudes, pieces)


def on_device(left_factor, right_factor, amplitudes, heights, owner_map, row_site):
    naux, bwidth, dpiece = right_factor.shape
    rows = left_factor.shape[0]
    formers = lax.axis_size("cd")
    place = lax.axis_index("cd").astype(jnp.int32).reshape(1)
    right = jnp.transpose(right_factor, (1, 2, 0)).reshape(bwidth * dpiece, naux)
    message = form(
        heights, place, owner_map.reshape(1, rows), row_site, left_factor, right, formers
    )
    arrived = lax.all_to_all(message, "cd", split_axis=0, concat_axis=0, tiled=True)
    coded = combine(arrived, lax.axis_size("ij"), amplitudes.shape[1], bwidth * dpiece)
    pieces = lax.all_to_all(coded, "ij", split_axis=0, concat_axis=0, tiled=True)
    partial = contract(amplitudes, pieces)
    shares = lax.all_to_all(partial, "cd", split_axis=0, concat_axis=0, tiled=True)
    return shares[:, 0, 0].sum(axis=0, keepdims=True)


def solution(mesh):
    placed = (
        P("cd", None),
        P(None, None, "ij"),
        P("ij", "cd", None),
        P("cd"),
        P("cd", None, None),
        P("cd", None),
    )
    return jax.shard_map(
        on_device, mesh=mesh, in_specs=placed, out_specs=P(("ij", "cd")), check_vma=False
    )
```

time: 116 us -> 94.4 us (0.81)
  blocking collectives: 43.2 us -> 79.9 us
  starting transfers between devices: 26.7 us -> 0 us
  waiting for transfers between devices: 18.6 us -> 0 us
  Pallas kernels: 0 us -> 12.7 us
  local copies, waits for them, and re-layouts: 11.1 us -> 0 us
  matrix products: 8.98 us -> 0 us
  other arithmetic: 6.35 us -> 0.65 us
    all_to_all x2 -> x3, blocking collectives: 43.2 us -> 79.9 us  [the longest x1 39 us: on_device(): lax.all_to_all(message, 'cd', split_axis=0, concat_axis=0, tiled=True)]
    all_to_all x2 -> x0, starting transfers between devices: 26.7 us -> none  [the longest x1 17.9 us: on_device(): lax.all_to_all(labels, 'cd', split_axis=0, concat_axis=0, tiled=True)]
    all_to_all x2 -> x0, waiting for transfers between devices: 18.6 us -> none  [the longest x1 16.4 us: on_device(): lax.all_to_all(outgoing, 'cd', split_axis=0, concat_axis=0, tiled=True)]
    pallas_call x0 -> x3, Pallas kernels: none -> 12.7 us  [the longest x1 8.24 us: form(): pl.pallas_call(form_kernel, grid=(KSTEPS,), in_specs=[pl.BlockSpec(memory...]
    dot_general x4 -> x0, matrix products: 8.98 us -> none  [the longest x1 4.13 us: on_device(): jnp.dot(dispatch.astype(jnp.bfloat16), panel, preferred_element_type=jnp....]
    unnamed x6 -> x0, local copies, waits for them, and re-layouts: 4.42 us -> none
    reshape x3 -> x0, local copies, waits for them, and re-layouts: 2.81 us -> none  [the longest x1 1.43 us: laid_out(): return jnp.moveaxis(pieces, 0, dim).reshape(dims)]
    all_to_all x2 -> x0, other arithmetic: 2.27 us -> none  [the longest x1 1.57 us: sent_to_all(): return lax.all_to_all(copies, axis, split_axis=0, concat_axis=0, tiled=True)]
  transfers between devices with their start and end apart: 2 -> 0, of which waited for: 2 -> 0; matrix products, arithmetic and copies ran while one was open for 8% -> 0% of each run, Pallas kernels for 0% -> 0%
where the time goes in v1:
time: 94.4 us; the launch traced here: 93.9 us
  blocking collectives  79.9 us (85%)
  Pallas kernels  12.7 us (13%)
    all_to_all x1, blocking collectives, on_device(): lax.all_to_all(message, 'cd', split_axis=0, concat_axis=0, tiled=True)  39 us
    all_to_all x1, blocking collectives, on_device(): lax.all_to_all(coded, 'ij', split_axis=0, concat_axis=0, tiled=True)  21.7 us
    all_to_all x1, blocking collectives, on_device(): lax.all_to_all(partial, 'cd', split_axis=0, concat_axis=0, tiled=True)  19.3 us
    pallas_call x1, Pallas kernels, form(): pl.pallas_call(form_kernel, grid=(KSTEPS,), in_specs=[pl.BlockSpec(memory...  8.24 us
    pallas_call x1, Pallas kernels, contract(): pl.pallas_call(contract_kernel, out_shape=jax.ShapeDtypeStruct((pairs * b...  2.47 us
    pallas_call x1, Pallas kernels, combine(): pl.pallas_call(combine_kernel, out_shape=jax.ShapeDtypeStruct((copies, ti...  1.97 us

profile of v1, /device:TPU:1, one launch (start us, length us, event | category | flops | bytes accessed | tf_op | source)
XLA Modules:
  0.0 93.9 jit_solution(2175037805791415472)
XLA Ops:
  0.7 8.2 %form.1 = bf16[48,40,128]{2,1,0:T(8,128)(2,1)} custom-call(s32[1]{0:T(128)S(6)} %copy.7.heights, s32[1]{0:T(128)} %bitcast.place, s32[1,512]{1,0:T(1,128)} %bitcast.7, s32[1,512]{1,0:T(1,128)} %sites.1, bf16[512,4096]{1,0:T(8,128)(2,1)} %left.1, bf16[256,4096]{1,0:T(8,128)(2,1)} %bitcast.6), custom_call_target="tpu_custom_call" | custom-call | tf_op jit(solution)/shard_map/form/pallas_call | solution.py:69
  8.9 39.0 %all_to_all.15.arrived = bf16[48,40,128]{2,1,0:T(8,128)(2,1)} all-to-all(bf16[48,40,128]{2,1,0:T(8,128)(2,1)} %form.1), channel_id=1, replica_groups=mesh['cd'=48,'ij'=16] {'cd'}, dimensions={0} | all-to-all | bytes 983040 | tf_op jit(solution)/shard_map/all_to_all | solution.py:183
  47.9 2.0 %combine.1 = s16[16,32,256]{2,1,0:T(8,128)(2,1)} custom-call(bf16[48,40,128]{2,1,0:T(8,128)(2,1)} %all_to_all.15.arrived), custom_call_target="tpu_custom_call" | custom-call | tf_op jit(solution)/shard_map/combine/pallas_call | solution.py:119
  49.8 21.7 %all_to_all.16.pieces = s16[16,32,256]{2,1,0:T(8,128)(2,1)} all-to-all(s16[16,32,256]{2,1,0:T(8,128)(2,1)} %combine.1), channel_id=1, replica_groups=mesh['cd'=48,'ij'=16] {'ij'}, dimensions={0} | all-to-all | bytes 524288 | tf_op jit(solution)/shard_map/all_to_all | solution.py:185
  71.5 2.5 %contract.1 = f32[48,1,128]{2,1,0:T(1,128)} custom-call(f32[12,24,1024]{2,1,0:T(8,128)} %amplitudes.1, s16[16,32,256]{2,1,0:T(8,128)(2,1)} %all_to_all.16.pieces), custom_call_target="tpu_custom_call" | custom-call | tf_op jit(solution)/shard_map/contract/pallas_call | solution.py:163
  74.0 19.3 %all_to_all.17 = f32[48,1,128]{2,1,0:T(1,128)S(1)} all-to-all(f32[48,1,128]{2,1,0:T(1,128)} %contract.1), channel_id=1, replica_groups=mesh['cd'=48,'ij'=16] {'cd'}, dimensions={0} | all-to-all | bytes 49152 | tf_op jit(solution)/shard_map/all_to_all | solution.py:187
  93.2 0.6 slice_reduce_fusion

commit v2 on v1

v2 whole, which is shorter than its diff:
```python
import functools

import jax
import jax.numpy as jnp
from jax import lax
from jax.experimental import pallas as pl
from jax.experimental.pallas import tpu as pltpu
from jax.sharding import PartitionSpec as P

SLOTS = 16
LANES = 128
KSTEPS = 8
QBITS = 14


def form_kernel(
    heights, place, owners_hbm, sites_hbm, left_hbm, right_hbm, out,
    owners, sites, left, right, acc, dispatch, sems, small_sems,
):
    rows, naux = left.shape
    cols = right.shape[0]
    block = naux // KSTEPS
    width = cols // LANES
    depth = width * SLOTS + 2
    formers = out.shape[0] // depth
    slots = formers * SLOTS
    small = (
        pltpu.make_async_copy(owners_hbm, owners, small_sems.at[0]),
        pltpu.make_async_copy(sites_hbm, sites, small_sems.at[1]),
    )
    for copy in small:
        copy.start()
    copies = []
    for k in range(KSTEPS):
        span = slice(k * block, (k + 1) * block)
        copies.append(
            (
                pltpu.make_async_copy(left_hbm.at[:, span], left.at[:, span], sems.at[0, k]),
                pltpu.make_async_copy(right_hbm.at[:, span], right.at[:, span], sems.at[1, k]),
            )
        )
        for copy in copies[-1]:
            copy.start()
    for copy in small:
        copy.wait()
    live = lax.broadcasted_iota(jnp.int32, (1, rows), 1) < heights[0]
    owner = jnp.where(live, owners[...], -1)
    hits = lax.broadcasted_iota(jnp.int32, (formers, rows), 0) == owner
    hits_f = jnp.where(hits, 1.0, 0.0)
    upto = lax.broadcasted_iota(jnp.int32, (rows, rows), 0) <= lax.broadcasted_iota(
        jnp.int32, (rows, rows), 1
    )
    upto = jnp.where(upto, 1.0, 0.0).astype(jnp.bfloat16)
    count = jnp.dot(hits_f.astype(jnp.bfloat16), upto, preferred_element_type=jnp.float32)
    within = jnp.sum(hits_f * count, axis=0, keepdims=True).astype(jnp.int32) - 1
    target = jnp.where(live, owner * SLOTS + within, -1)
    lane = within + (place[0] % (LANES // SLOTS)) * SLOTS
    at_lane = lax.broadcasted_iota(jnp.int32, (LANES, rows), 0) == lane
    at_lane = jnp.where(at_lane, 1.0, 0.0).astype(jnp.bfloat16)
    tagged = hits_f * (sites[...] + 1).astype(jnp.float32)
    tags = lax.dot_general(
        tagged.astype(jnp.bfloat16),
        at_lane,
        (((1,), (1,)), ((), ())),
        preferred_element_type=jnp.float32,
    )
    for t in range(formers):
        tag = jnp.broadcast_to(tags[t : t + 1, :], (2, LANES))
        out[t * depth + width * SLOTS : (t + 1) * depth, :] = tag.astype(jnp.bfloat16)
    chosen = lax.broadcasted_iota(jnp.int32, (slots, rows), 0) == target
    dispatch[...] = jnp.where(chosen, 1.0, 0.0).astype(jnp.bfloat16)
    for k in range(KSTEPS):
        span = slice(k * block, (k + 1) * block)
        for copy in copies[k]:
            copy.wait()
        part = lax.dot_general(
            left[:, span],
            right[:, span],
            (((1,), (1,)), ((), ())),
            preferred_element_type=jnp.float32,
        )
        acc[...] = part if k == 0 else acc[...] + part
    panel = acc[...].astype(jnp.bfloat16)
    moved = jnp.dot(dispatch[...], panel, preferred_element_type=jnp.float32)
    moved = moved.astype(jnp.bfloat16)
    for t in range(formers):
        for part in range(width):
            at = t * depth + part * SLOTS
            piece = moved[t * SLOTS : (t + 1) * SLOTS, part * LANES : (part + 1) * LANES]
            out[at : at + SLOTS, :] = piece


def form(heights, place, owners, sites, left, right, formers):
    rows, naux = left.shape
    cols = right.shape[0]
    depth = cols // LANES * SLOTS + 2
    return pl.pallas_call(
        form_kernel,
        in_specs=[
            pl.BlockSpec(memory_space=pltpu.SMEM),
            pl.BlockSpec(memory_space=pltpu.SMEM),
            pl.BlockSpec(memory_space=pl.ANY),
            pl.BlockSpec(memory_space=pl.ANY),
            pl.BlockSpec(memory_space=pl.ANY),
            pl.BlockSpec(memory_space=pl.ANY),
        ],
        out_specs=pl.BlockSpec(memory_space=pltpu.VMEM),
        out_shape=pltpu.VMEM((formers * depth, LANES), jnp.bfloat16),
        scratch_shapes=[
            pltpu.VMEM((1, rows), jnp.int32),
            pltpu.VMEM((1, rows), jnp.int32),
            pltpu.VMEM((rows, naux), jnp.bfloat16),
            pltpu.VMEM((cols, naux), jnp.bfloat16),
            pltpu.VMEM((rows, cols), jnp.float32),
            pltpu.VMEM((formers * SLOTS, rows), jnp.bfloat16),
            pltpu.SemaphoreType.DMA((2, KSTEPS)),
            pltpu.SemaphoreType.DMA((2,)),
        ],
        name="form",
    )(heights, place, owners, sites, left, right)


def combine_kernel(arrived, out, *, formers, copies):
    depth = arrived.shape[0] // formers
    width = depth // SLOTS
    piece = out.shape[0] // copies
    tile = (piece - 2) // width
    group = LANES // SLOTS
    site = lax.broadcasted_iota(jnp.int32, (tile, LANES), 0).astype(jnp.float32) + 1.0
    pickers = []
    for g in range(formers // group):
        tag = jnp.zeros((2, LANES), jnp.float32)
        for f in range(g * group, (g + 1) * group):
            at = f * depth + width * SLOTS
            tag = tag + arrived[at : at + 2, :].astype(jnp.float32)
        pickers.append(jnp.where(tag[:1] == site, 1.0, 0.0).astype(jnp.bfloat16))
    picker = jnp.concatenate(pickers, axis=1)
    powers = []
    for part in range(width):
        rows = []
        for f in range(formers):
            at = f * depth + part * SLOTS
            rows.append(arrived[at : at + SLOTS, :])
        rows = jnp.concatenate(rows, axis=0)
        sums = jnp.dot(picker, rows, preferred_element_type=jnp.float32)
        top = jnp.maximum(jnp.max(jnp.abs(sums), axis=0, keepdims=True), 2.0**-100)
        power = jnp.ceil(jnp.log(top) * 1.4426950408889634)
        coded = jnp.round(sums * jnp.exp2(QBITS - power)).astype(jnp.int32).astype(jnp.int16)
        powers.append(power)
        for copy in range(copies):
            at = copy * piece + part * tile
            out[at : at + tile, :] = coded
    powers = jnp.concatenate(powers, axis=0).astype(jnp.int32).astype(jnp.int16)
    for copy in range(copies):
        at = copy * piece + width * tile
        out[at : at + width, :] = powers


def combine(arrived, formers, copies, tile, cols):
    width = cols // LANES
    return pl.pallas_call(
        functools.partial(combine_kernel, formers=formers, copies=copies),
        in_specs=[pl.BlockSpec(memory_space=pltpu.VMEM)],
        out_specs=pl.BlockSpec(memory_space=pltpu.VMEM),
        out_shape=pltpu.VMEM((copies * (width * tile + 2), LANES), jnp.int16),
        name="combine",
    )(pltpu.with_memory_space_constraint(arrived, pltpu.VMEM))


def contract_kernel(amplitudes, pieces, out, sums, ends, *, count):
    pairs, tile, _ = amplitudes.shape
    piece = pieces.shape[0] // count
    width = (piece - 2) // tile
    dpiece = LANES // 2
    bwidth = width * 2
    low = lax.broadcasted_iota(jnp.int32, (tile, LANES), 1) < dpiece
    for two in range(count // 2):
        span = slice(two * LANES, (two + 1) * LANES)
        both = []
        for j in (2 * two, 2 * two + 1):
            at = j * piece
            powers = pieces[at + width * tile : at + width * tile + 2, :]
            powers = jnp.exp2(powers.astype(jnp.int32).astype(jnp.float32) - QBITS)
            for half in range(width):
                whole = pieces[at + half * tile : at + (half + 1) * tile, :]
                whole = whole.astype(jnp.int32).astype(jnp.float32)
                both.append(whole * powers[half : half + 1])
        for half in range(width):
            a, b = both[half], both[width + half]
            sums[2 * half, :, span] = jnp.where(low, a, pltpu.roll(b, dpiece, 1))
            sums[2 * half + 1, :, span] = jnp.where(low, pltpu.roll(a, dpiece, 1), b)
    some = 6
    for first in range(0, pairs, some):
        totals = [[jnp.zeros((8, LANES), jnp.float32) for _ in range(bwidth)] for _ in range(some)]
        for c in range(0, tile, 8):
            for d in range(0, amplitudes.shape[2], LANES):
                s = [sums[b, c : c + 8, d : d + LANES] for b in range(bwidth)]
                for i in range(some):
                    t = amplitudes[first + i, c : c + 8, d : d + LANES]
                    for b in range(bwidth):
                        totals[i][b] = totals[i][b] + t * s[b]
        for i in range(some):
            for b in range(bwidth):
                at = (first + i) * bwidth + b
                ends[at : at + 1, :] = jnp.sum(totals[i][b], axis=0, keepdims=True)
    total = jnp.sum(ends[...], axis=1, keepdims=True)
    out[...] = jnp.broadcast_to(total, ends.shape)[:, None, :]


def contract(amplitudes, pieces, count, bwidth):
    pairs, tile, virt = amplitudes.shape
    return pl.pallas_call(
        functools.partial(contract_kernel, count=count),
        in_specs=[pl.BlockSpec(memory_space=pltpu.VMEM), pl.BlockSpec(memory_space=pltpu.VMEM)],
        out_specs=pl.BlockSpec(memory_space=pltpu.VMEM),
        out_shape=pltpu.VMEM((pairs * bwidth, 1, LANES), jnp.float32),
        scratch_shapes=[
            pltpu.VMEM((bwidth, tile, virt), jnp.float32),
            pltpu.VMEM((pairs * bwidth, LANES), jnp.float32),
        ],
        name="contract",
    )(
        pltpu.with_memory_space_constraint(amplitudes, pltpu.VMEM),
        pltpu.with_memory_space_constraint(pieces, pltpu.VMEM),
    )


def exchanged(rows, axis):
    count = lax.axis_size(axis)
    tiles = rows.reshape(count, rows.shape[0] // (2 * count), 2, LANES)
    tiles = lax.all_to_all(tiles, axis, split_axis=0, concat_axis=0, tiled=True)
    return tiles.reshape(rows.shape)


def on_device(left_factor, right_factor, amplitudes, heights, owner_map, row_site):
    naux, bwidth, dpiece = right_factor.shape
    rows = left_factor.shape[0]
    formers = lax.axis_size("cd")
    place = lax.axis_index("cd").astype(jnp.int32).reshape(1)
    right = jnp.transpose(right_factor, (1, 2, 0)).reshape(bwidth * dpiece, naux)
    message = form(
        heights, place, owner_map.reshape(1, rows), row_site, left_factor, right, formers
    )
    arrived = exchanged(message, "cd")
    parts = lax.axis_size("ij")
    coded = combine(arrived, formers, parts, amplitudes.shape[1], bwidth * dpiece)
    pieces = exchanged(coded, "ij")
    partial = contract(amplitudes, pieces, parts, bwidth)
    shares = lax.all_to_all(partial, "cd", split_axis=0, concat_axis=0, tiled=True)
    return shares[:, 0, 0].sum(axis=0, keepdims=True)


def solution(mesh):
    placed = (
        P("cd", None),
        P(None, None, "ij"),
        P("ij", "cd", None),
        P("cd"),
        P("cd", None, None),
        P("cd", None),
    )
    return jax.shard_map(
        on_device, mesh=mesh, in_specs=placed, out_specs=P(("ij", "cd")), check_vma=False
    )
```

time: 94.4 us -> 84.9 us (0.90)
  Pallas kernels: 12.7 us -> 7.48 us
  blocking collectives: 79.9 us -> 75.8 us
    pallas_call x3, Pallas kernels: 12.7 us -> 7.48 us  [the longest x1 6.65 us: form(): pl.pallas_call(form_kernel, in_specs=[pl.BlockSpec(memory_space=pltpu.SME...]
    all_to_all x2, blocking collectives: 60.6 us -> 56.6 us  [exchanged(): tiles = lax.all_to_all(tiles, axis, split_axis=0, concat_axis=0, tiled=True)]
where the time goes in v2:
time: 84.9 us; the launch traced here: 84.6 us
  blocking collectives  75.8 us (89%)
  Pallas kernels  7.48 us (9%)
    all_to_all x2, blocking collectives, exchanged(): tiles = lax.all_to_all(tiles, axis, split_axis=0, concat_axis=0, tiled=True)  56.6 us
    all_to_all x1, blocking collectives, on_device(): lax.all_to_all(partial, 'cd', split_axis=0, concat_axis=0, tiled=True)  19.3 us
    pallas_call x1, Pallas kernels, form(): pl.pallas_call(form_kernel, in_specs=[pl.BlockSpec(memory_space=pltpu.SME...  6.65 us

profile of v2, /device:TPU:1, one launch (start us, length us, event | category | flops | bytes accessed | tf_op | source)
XLA Modules:
  0.0 84.6 jit_solution(1434356981466268880)
XLA Ops:
  0.7 6.7 %form.1 = bf16[1632,128]{1,0:T(8,128)(2,1)S(1)} custom-call(s32[1]{0:T(128)S(6)} %copy.7.heights, s32[1]{0:T(128)} %bitcast.place, s32[1,512]{1,0:T(1,128)} %bitcast.15, s32[1,512]{1,0:T(1,128)} %sites_hbm.1, bf16[512,4096]{1,0:T(8,128)(2,1)} %left_hbm.1, bf16[256,4096]{1,0:T(8,128)(2,1)} %bitcast.14), custom_call_target="tpu_custom_call" | custom-call | tf_op jit(solution)/shard_map/form/pallas_call | solution.py:97
  7.3 0.0 copy-start
  7.3 36.4 %all_to_all.15 = bf16[48,17,2,128]{3,2,1,0:T(2,128)(2,1)S(1)} all-to-all(bf16[48,17,2,128]{3,2,1,0:T(2,128)(2,1)S(1)} %bitcast.10), channel_id=1, replica_groups=mesh['cd'=48,'ij'=16] {'cd'}, dimensions={0} | all-to-all | bytes 835584 | tf_op jit(solution)/shard_map/all_to_all | solution.py:231
  43.8 0.2 combine.1
  44.0 20.1 %all_to_all.16 = s16[16,25,2,128]{3,2,1,0:T(2,128)(2,1)S(1)} all-to-all(s16[16,25,2,128]{3,2,1,0:T(2,128)(2,1)S(1)} %bitcast.12), channel_id=1, replica_groups=mesh['cd'=48,'ij'=16] {'ij'}, dimensions={0} | all-to-all | bytes 409600 | tf_op jit(solution)/shard_map/all_to_all | solution.py:231
  64.1 0.0 copy-done
  64.1 0.6 contract.1
  64.7 19.3 %all_to_all.17 = f32[48,1,128]{2,1,0:T(1,128)S(1)} all-to-all(f32[48,1,128]{2,1,0:T(1,128)S(1)} %contract.1), channel_id=1, replica_groups=mesh['cd'=48,'ij'=16] {'cd'}, dimensions={0} | all-to-all | bytes 49152 | tf_op jit(solution)/shard_map/all_to_all | solution.py:249
  84.0 0.6 slice_reduce_fusion
Async XLA Ops:
  7.3 56.8 %copy-start = (f32[12,24,1024]{2,1,0:T(8,128)S(1)}, f32[12,24,1024]{2,1,0:T(8,128)}, u32[]{:S(2)}) copy-start(f32[12,24,1024]{2,1,0:T(8,128)} %amplitudes.1) | copy-start | bytes 3538948

commit v3 on v2

--- a/solution.py
+++ b/solution.py
@@ -9,7 +9,9 @@
 
 SLOTS = 16
 LANES = 128
-KSTEPS = 8
+EARLY = 3
+CORES = 2
+SIDE = 2
 QBITS = 14
 
 
@@ -19,7 +21,6 @@
 ):
     rows, naux = left.shape
     cols = right.shape[0]
-    block = naux // KSTEPS
     width = cols // LANES
     depth = width * SLOTS + 2
     formers = out.shape[0] // depth
@@ -30,21 +31,27 @@
     )
     for copy in small:
         copy.start()
+    spans = [slice(0, naux * EARLY // 4), slice(naux * EARLY // 4, naux)]
     copies = []
-    for k in range(KSTEPS):
-        span = slice(k * block, (k + 1) * block)
+    for k, span in enumerate(spans):
         copies.append(
             (
                 pltpu.make_async_copy(left_hbm.at[:, span], left.at[:, span], sems.at[0, k]),
                 pltpu.make_async_copy(right_hbm.at[:, span], right.at[:, span], sems.at[1, k]),
             )
         )
-        for copy in copies[-1]:
-            copy.start()
+    for copy in copies[0]:
+        copy.start()
     for copy in small:
         copy.wait()
     live = lax.broadcasted_iota(jnp.int32, (1, rows), 1) < heights[0]
-    owner = jnp.where(live, owners[...], -1)
+    planes = formers // (CORES * SIDE)
+    tile = owners[...]
+    side = jnp.where(tile >= planes * CORES, 1, 0)
+    inner = tile - side * planes * CORES
+    plane = lax.shift_right_logical(inner, 1)
+    owner = (side * CORES + (inner & 1)) * planes + plane
+    owner = jnp.where(live, owner, -1)
     hits = lax.broadcasted_iota(jnp.int32, (formers, rows), 0) == owner
     hits_f = jnp.where(hits, 1.0, 0.0)
     upto = lax.broadcasted_iota(jnp.int32, (rows, rows), 0) <= lax.broadcasted_iota(
@@ -54,7 +61,9 @@
     count = jnp.dot(hits_f.astype(jnp.bfloat16), upto, preferred_element_type=jnp.float32)
     within = jnp.sum(hits_f * count, axis=0, keepdims=True).astype(jnp.int32) - 1
     target = jnp.where(live, owner * SLOTS + within, -1)
-    lane = within + (place[0] % (LANES // SLOTS)) * SLOTS
+    mine = jnp.where(place[0] >= planes * CORES, CORES, 0) + (place[0] & 1)
+    run = (mine * planes + plane) & (LANES // SLOTS - 1)
+    lane = jnp.where(live, within + run * SLOTS, -1)
     at_lane = lax.broadcasted_iota(jnp.int32, (LANES, rows), 0) == lane
     at_lane = jnp.where(at_lane, 1.0, 0.0).astype(jnp.bfloat16)
     tagged = hits_f * (sites[...] + 1).astype(jnp.float32)
@@ -69,8 +78,9 @@
         out[t * depth + width * SLOTS : (t + 1) * depth, :] = tag.astype(jnp.bfloat16)
     chosen = lax.broadcasted_iota(jnp.int32, (slots, rows), 0) == target
     dispatch[...] = jnp.where(chosen, 1.0, 0.0).astype(jnp.bfloat16)
-    for k in range(KSTEPS):
-        span = slice(k * block, (k + 1) * block)
+    for copy in copies[1]:
+        copy.start()
+    for k, span in enumerate(spans):
         for copy in copies[k]:
             copy.wait()
         part = lax.dot_general(
@@ -113,39 +123,93 @@
             pltpu.VMEM((cols, naux), jnp.bfloat16),
             pltpu.VMEM((rows, cols), jnp.float32),
             pltpu.VMEM((formers * SLOTS, rows), jnp.bfloat16),
-            pltpu.SemaphoreType.DMA((2, KSTEPS)),
+            pltpu.SemaphoreType.DMA((2, 2)),
             pltpu.SemaphoreType.DMA((2,)),
         ],
         name="form",
     )(heights, place, owners, sites, left, right)
 
 
-def combine_kernel(arrived, out, *, formers, copies):
-    depth = arrived.shape[0] // formers
+def encoded(sums):
+    top = jnp.maximum(jnp.max(jnp.abs(sums), axis=0, keepdims=True), 2.0**-100)
+    power = jnp.ceil(jnp.log(top) * 1.4426950408889634)
+    return jnp.round(sums * jnp.exp2(QBITS - power)).astype(jnp.int32).astype(jnp.int16), power
+
+
+def decoded(piece, at, tile, width):
+    powers = piece[at + width * tile : at + width * tile + 2, :]
+    powers = jnp.exp2(powers.astype(jnp.int32).astype(jnp.float32) - QBITS)
+    parts = []
+    for part in range(width):
+        whole = piece[at + part * tile : at + (part + 1) * tile, :]
+        parts.append(whole.astype(jnp.int32).astype(jnp.float32) * powers[part : part + 1])
+    return parts
+
+
+def collate_kernel(arrived, out, *, runs, planes):
+    depth = arrived.shape[0] // runs
     width = depth // SLOTS
-    piece = out.shape[0] // copies
+    piece = out.shape[0] // planes
     tile = (piece - 2) // width
     group = LANES // SLOTS
-    site = lax.broadcasted_iota(jnp.int32, (tile, LANES), 0).astype(jnp.float32) + 1.0
-    pickers = []
-    for g in range(formers // group):
+    step = 32.0
+    codes = []
+    for g in range(runs // group):
         tag = jnp.zeros((2, LANES), jnp.float32)
-        for f in range(g * group, (g + 1) * group):
-            at = f * depth + width * SLOTS
+        for r in range(g * group, (g + 1) * group):
+            at = r * depth + width * SLOTS
             tag = tag + arrived[at : at + 2, :].astype(jnp.float32)
-        pickers.append(jnp.where(tag[:1] == site, 1.0, 0.0).astype(jnp.bfloat16))
-    picker = jnp.concatenate(pickers, axis=1)
+        run = lax.shift_right_logical(lax.broadcasted_iota(jnp.int32, (1, LANES), 1), 4) + g * group
+        plane = run
+        for wrap in range(planes, runs, planes):
+            plane = plane - jnp.where(run >= wrap, planes, 0)
+        codes.append(jnp.where(tag[:1] > 0.0, tag[:1] + step * plane.astype(jnp.float32), 0.0))
+    codes = jnp.concatenate(codes, axis=1)
+    site = lax.broadcasted_iota(jnp.int32, (tile, codes.shape[1]), 0).astype(jnp.float32) + 1.0
+    pickers = [jnp.where(codes == site + step * z, 1.0, 0.0) for z in range(planes)]
+    picker = jnp.concatenate(pickers, axis=0).astype(jnp.bfloat16)
+    rows = []
+    for r in range(runs):
+        parts = []
+        for part in range(width):
+            at = r * depth + part * SLOTS
+            parts.append(arrived[at : at + SLOTS, :])
+        rows.append(jnp.concatenate(parts, axis=1))
+    rows = jnp.concatenate(rows, axis=0)
+    sums = jnp.dot(picker, rows, preferred_element_type=jnp.float32)
+    for z in range(planes):
+        powers = []
+        for part in range(width):
+            coded, power = encoded(
+                sums[z * tile : (z + 1) * tile, part * LANES : (part + 1) * LANES]
+            )
+            at = z * piece + part * tile
+            out[at : at + tile, :] = coded
+            powers.append(power)
+        powers = jnp.concatenate(powers, axis=0).astype(jnp.int32).astype(jnp.int16)
+        at = z * piece + width * tile
+        out[at : at + width, :] = powers
+
+
+def collate(arrived, runs, planes, tile, cols):
+    return pl.pallas_call(
+        functools.partial(collate_kernel, runs=runs, planes=planes),
+        in_specs=[pl.BlockSpec(memory_space=pltpu.VMEM)],
+        out_specs=pl.BlockSpec(memory_space=pltpu.VMEM),
+        out_shape=pltpu.VMEM((planes * (cols // LANES * tile + 2), LANES), jnp.int16),
+        name="collate",
+    )(pltpu.with_memory_space_constraint(arrived, pltpu.VMEM))
+
+
+def combine_kernel(arrived, out, *, planes, copies, tile, width):
+    piece = width * tile + 2
+    totals = decoded(arrived, 0, tile, width)
+    for z in range(1, planes):
+        parts = decoded(arrived, z * piece, tile, width)
+        totals = [total + part for total, part in zip(totals, parts)]
     powers = []
     for part in range(width):
-        rows = []
-        for f in range(formers):
-            at = f * depth + part * SLOTS
-            rows.append(arrived[at : at + SLOTS, :])
-        rows = jnp.concatenate(rows, axis=0)
-        sums = jnp.dot(picker, rows, preferred_element_type=jnp.float32)
-        top = jnp.maximum(jnp.max(jnp.abs(sums), axis=0, keepdims=True), 2.0**-100)
-        power = jnp.ceil(jnp.log(top) * 1.4426950408889634)
-        coded = jnp.round(sums * jnp.exp2(QBITS - power)).astype(jnp.int32).astype(jnp.int16)
+        coded, power = encoded(totals[part])
         powers.append(power)
         for copy in range(copies):
             at = copy * piece + part * tile
@@ -156,10 +220,10 @@
         out[at : at + width, :] = powers
 
 
-def combine(arrived, formers, copies, tile, cols):
+def combine(arrived, planes, copies, tile, cols):
     width = cols // LANES
     return pl.pallas_call(
-        functools.partial(combine_kernel, formers=formers, copies=copies),
+        functools.partial(combine_kernel, planes=planes, copies=copies, tile=tile, width=width),
         in_specs=[pl.BlockSpec(memory_space=pltpu.VMEM)],
         out_specs=pl.BlockSpec(memory_space=pltpu.VMEM),
         out_shape=pltpu.VMEM((copies * (width * tile + 2), LANES), jnp.int16),
@@ -178,13 +242,7 @@
         span = slice(two * LANES, (two + 1) * LANES)
         both = []
         for j in (2 * two, 2 * two + 1):
-            at = j * piece
-            powers = pieces[at + width * tile : at + width * tile + 2, :]
-            powers = jnp.exp2(powers.astype(jnp.int32).astype(jnp.float32) - QBITS)
-            for half in range(width):
-                whole = pieces[at + half * tile : at + (half + 1) * tile, :]
-                whole = whole.astype(jnp.int32).astype(jnp.float32)
-                both.append(whole * powers[half : half + 1])
+            both += decoded(pieces, j * piece, tile, width)
         for half in range(width):
             a, b = both[half], both[width + half]
             sums[2 * half, :, span] = jnp.where(low, a, pltpu.roll(b, dpiece, 1))
@@ -225,25 +283,38 @@
     )
 
 
-def exchanged(rows, axis):
-    count = lax.axis_size(axis)
+def exchanged(rows, axis, groups=None):
+    count = len(groups[0]) if groups else lax.axis_size(axis)
     tiles = rows.reshape(count, rows.shape[0] // (2 * count), 2, LANES)
-    tiles = lax.all_to_all(tiles, axis, split_axis=0, concat_axis=0, tiled=True)
+    tiles = lax.all_to_all(
+        tiles, axis, split_axis=0, concat_axis=0, tiled=True, axis_index_groups=groups
+    )
     return tiles.reshape(rows.shape)
 
 
 def on_device(left_factor, right_factor, amplitudes, heights, owner_map, row_site):
     naux, bwidth, dpiece = right_factor.shape
+    cols = bwidth * dpiece
     rows = left_factor.shape[0]
+    tile = amplitudes.shape[1]
     formers = lax.axis_size("cd")
+    parts = lax.axis_size("ij")
+    planes = formers // (CORES * SIDE)
+    at = [
+        [[(s * planes + z) * CORES + c for c in range(CORES)] for z in range(planes)]
+        for s in range(SIDE)
+    ]
+    beside = [[at[s][z][c] for s in range(SIDE) for c in range(CORES)] for z in range(planes)]
+    along = [[at[s][z][c] for z in range(planes)] for s in range(SIDE) for c in range(CORES)]
     place = lax.axis_index("cd").astype(jnp.int32).reshape(1)
-    right = jnp.transpose(right_factor, (1, 2, 0)).reshape(bwidth * dpiece, naux)
+    right = jnp.transpose(right_factor, (1, 2, 0)).reshape(cols, naux)
     message = form(
         heights, place, owner_map.reshape(1, rows), row_site, left_factor, right, formers
     )
-    arrived = exchanged(message, "cd")
-    parts = lax.axis_size("ij")
-    coded = combine(arrived, formers, parts, amplitudes.shape[1], bwidth * dpiece)
+    arrived = exchanged(message, "cd", beside)
+    collated = collate(arrived, formers, planes, tile, cols)
+    planar = exchanged(collated, "cd", along)
+    coded = combine(planar, planes, parts, tile, cols)
     pieces = exchanged(coded, "ij")
     partial = contract(amplitudes, pieces, parts, bwidth)
     shares = lax.all_to_all(partial, "cd", split_axis=0, concat_axis=0, tiled=True)

time: 84.9 us -> 82 us (0.966)
  Pallas kernels: 7.48 us -> 5.75 us
  blocking collectives: 75.8 us -> 74.7 us
    pallas_call x1, Pallas kernels: 6.65 us -> 4.66 us  [form(): pl.pallas_call(form_kernel, in_specs=[pl.BlockSpec(memory_space=pltpu.SME...]
    all_to_all x1, blocking collectives: 19.3 us -> 17.3 us  [on_device(): lax.all_to_all(partial, 'cd', split_axis=0, concat_axis=0, tiled=True)]
    all_to_all x2 -> x3, blocking collectives: 56.6 us -> 57.4 us  [exchanged(): lax.all_to_all(tiles, axis, split_axis=0, concat_axis=0, tiled=True, axis...]
where the time goes in v3:
time: 82 us; the launch traced here: 81.8 us
  blocking collectives  74.7 us (91%)
  Pallas kernels  5.75 us (7%)
    all_to_all x3, blocking collectives, exchanged(): lax.all_to_all(tiles, axis, split_axis=0, concat_axis=0, tiled=True, axis...  57.4 us
    all_to_all x1, blocking collectives, on_device(): lax.all_to_all(partial, 'cd', split_axis=0, concat_axis=0, tiled=True)  17.3 us
    pallas_call x1, Pallas kernels, form(): pl.pallas_call(form_kernel, in_specs=[pl.BlockSpec(memory_space=pltpu.SME...  4.66 us

profile of v3, /device:TPU:1, one launch (start us, length us, event | category | flops | bytes accessed | tf_op | source)
XLA Modules:
  0.0 81.8 jit_solution(14267961237152495435)
XLA Ops:
  0.7 4.7 %form.1 = bf16[1632,128]{1,0:T(8,128)(2,1)S(1)} custom-call(s32[1]{0:T(128)S(6)} %copy.7.heights, s32[1]{0:T(128)} %bitcast.place, s32[1,512]{1,0:T(1,128)} %bitcast.19, s32[1,512]{1,0:T(1,128)} %sites_hbm.1, bf16[512,4096]{1,0:T(8,128)(2,1)} %left_hbm.1, bf16[256,4096]{1,0:T(8,128)(2,1)} %bitcast.18), custom_call_target="tpu_custom_call" | custom-call | tf_op jit(solution)/shard_map/form/pallas_call | solution.py:107
  5.3 0.0 copy-start
  5.3 20.1 %all_to_all.20 = bf16[4,204,2,128]{3,2,1,0:T(2,128)(2,1)S(1)} all-to-all(bf16[4,204,2,128]{3,2,1,0:T(2,128)(2,1)S(1)} %bitcast.12), channel_id=1, replica_groups={{0,16,384,400},{32,48,416,432},{64,80,448,464},{96,112,480,496},{128,14..., dimensions={0} | all-to-all | bytes 835584 | tf_op jit(solution)/shard_map/all_to_all | solution.py:289
  25.5 0.4 collate.1
  25.8 17.7 %all_to_all.21 = s16[12,25,2,128]{3,2,1,0:T(2,128)(2,1)S(1)} all-to-all(s16[12,25,2,128]{3,2,1,0:T(2,128)(2,1)S(1)} %bitcast.16), channel_id=1, replica_groups={{0,32,64,96,128,160,192,224,256,288,320,352},{16,48,80,112,144,176,208,..., dimensions={0} | all-to-all | bytes 307200 | tf_op jit(solution)/shard_map/all_to_all | solution.py:289
  43.5 0.1 combine.1
  43.6 19.6 %all_to_all.22 = s16[16,25,2,128]{3,2,1,0:T(2,128)(2,1)S(1)} all-to-all(s16[16,25,2,128]{3,2,1,0:T(2,128)(2,1)S(1)} %bitcast.14), channel_id=1, replica_groups=mesh['cd'=48,'ij'=16] {'ij'}, dimensions={0} | all-to-all | bytes 409600 | tf_op jit(solution)/shard_map/all_to_all | solution.py:289
  63.2 0.0 copy-done
  63.2 0.6 contract.1
  63.8 17.3 %all_to_all.23 = f32[48,1,128]{2,1,0:T(1,128)S(1)} all-to-all(f32[48,1,128]{2,1,0:T(1,128)S(1)} %contract.1), channel_id=1, replica_groups=mesh['cd'=48,'ij'=16] {'cd'}, dimensions={0} | all-to-all | bytes 49152 | tf_op jit(solution)/shard_map/all_to_all | solution.py:320
  81.1 0.6 slice_reduce_fusion
Async XLA Ops:
  5.3 57.9 %copy-start = (f32[12,24,1024]{2,1,0:T(8,128)S(1)}, f32[12,24,1024]{2,1,0:T(8,128)}, u32[]{:S(2)}) copy-start(f32[12,24,1024]{2,1,0:T(8,128)} %amplitudes.1) | copy-start | bytes 3538948

commit v4 on v3

--- a/solution.py
+++ b/solution.py
@@ -12,7 +12,24 @@
 EARLY = 3
 CORES = 2
 SIDE = 2
+PLANE_TURN = 9
+PART_STEP = 5
+PART_TURN = 4
+LAST_TURN = 16
 QBITS = 14
+
+
+def plane_order(planes):
+    half = planes // 2
+    return [(at + PLANE_TURN) % planes for step in range(half) for at in (step, step + half)]
+
+
+def part_order(pairs):
+    return [(PART_STEP * step + PART_TURN) % pairs for step in range(pairs)]
+
+
+def last_order(formers):
+    return [(at + LAST_TURN) % formers for at in range(formers)]
 
 
 def form_kernel(
@@ -22,8 +39,10 @@
     rows, naux = left.shape
     cols = right.shape[0]
     width = cols // LANES
-    depth = width * SLOTS + 2
-    formers = out.shape[0] // depth
+    beside = CORES * SIDE
+    depth = out.shape[0] // beside
+    planes = (depth - SLOTS) // (width * SLOTS)
+    formers = planes * beside
     slots = formers * SLOTS
     small = (
         pltpu.make_async_copy(owners_hbm, owners, small_sems.at[0]),
@@ -45,13 +64,12 @@
     for copy in small:
         copy.wait()
     live = lax.broadcasted_iota(jnp.int32, (1, rows), 1) < heights[0]
-    planes = formers // (CORES * SIDE)
     tile = owners[...]
     side = jnp.where(tile >= planes * CORES, 1, 0)
     inner = tile - side * planes * CORES
     plane = lax.shift_right_logical(inner, 1)
-    owner = (side * CORES + (inner & 1)) * planes + plane
-    owner = jnp.where(live, owner, -1)
+    peer = side * CORES + (inner & 1)
+    owner = jnp.where(live, peer * planes + plane, -1)
     hits = lax.broadcasted_iota(jnp.int32, (formers, rows), 0) == owner
     hits_f = jnp.where(hits, 1.0, 0.0)
     upto = lax.broadcasted_iota(jnp.int32, (rows, rows), 0) <= lax.broadcasted_iota(
@@ -62,20 +80,21 @@
     within = jnp.sum(hits_f * count, axis=0, keepdims=True).astype(jnp.int32) - 1
     target = jnp.where(live, owner * SLOTS + within, -1)
     mine = jnp.where(place[0] >= planes * CORES, CORES, 0) + (place[0] & 1)
-    run = (mine * planes + plane) & (LANES // SLOTS - 1)
-    lane = jnp.where(live, within + run * SLOTS, -1)
+    run = ((mine * planes) & (LANES // SLOTS - 1)) + plane
+    lane = jnp.where(live, within + (run & (LANES // SLOTS - 1)) * SLOTS, -1)
     at_lane = lax.broadcasted_iota(jnp.int32, (LANES, rows), 0) == lane
     at_lane = jnp.where(at_lane, 1.0, 0.0).astype(jnp.bfloat16)
-    tagged = hits_f * (sites[...] + 1).astype(jnp.float32)
+    line = peer * SLOTS + lax.shift_right_logical(run, 3)
+    at_line = lax.broadcasted_iota(jnp.int32, (beside * SLOTS, rows), 0) == line
+    tagged = jnp.where(at_line, (sites[...] + 1).astype(jnp.float32), 0.0)
     tags = lax.dot_general(
         tagged.astype(jnp.bfloat16),
         at_lane,
         (((1,), (1,)), ((), ())),
         preferred_element_type=jnp.float32,
-    )
-    for t in range(formers):
-        tag = jnp.broadcast_to(tags[t : t + 1, :], (2, LANES))
-        out[t * depth + width * SLOTS : (t + 1) * depth, :] = tag.astype(jnp.bfloat16)
+    ).astype(jnp.bfloat16)
+    for q in range(beside):
+        out[(q + 1) * depth - SLOTS : (q + 1) * depth, :] = tags[q * SLOTS : (q + 1) * SLOTS]
     chosen = lax.broadcasted_iota(jnp.int32, (slots, rows), 0) == target
     dispatch[...] = jnp.where(chosen, 1.0, 0.0).astype(jnp.bfloat16)
     for copy in copies[1]:
@@ -95,7 +114,7 @@
     moved = moved.astype(jnp.bfloat16)
     for t in range(formers):
         for part in range(width):
-            at = t * depth + part * SLOTS
+            at = t // planes * depth + (t % planes * width + part) * SLOTS
             piece = moved[t * SLOTS : (t + 1) * SLOTS, part * LANES : (part + 1) * LANES]
             out[at : at + SLOTS, :] = piece
 
@@ -103,7 +122,7 @@
 def form(heights, place, owners, sites, left, right, formers):
     rows, naux = left.shape
     cols = right.shape[0]
-    depth = cols // LANES * SLOTS + 2
+    size = (cols // LANES * formers + CORES * SIDE) * SLOTS
     return pl.pallas_call(
         form_kernel,
         in_specs=[
@@ -115,7 +134,7 @@
             pl.BlockSpec(memory_space=pl.ANY),
         ],
         out_specs=pl.BlockSpec(memory_space=pltpu.VMEM),
-        out_shape=pltpu.VMEM((formers * depth, LANES), jnp.bfloat16),
+        out_shape=pltpu.VMEM((size, LANES), jnp.bfloat16),
         scratch_shapes=[
             pltpu.VMEM((1, rows), jnp.int32),
             pltpu.VMEM((1, rows), jnp.int32),
@@ -146,24 +165,27 @@
     return parts
 
 
-def collate_kernel(arrived, out, *, runs, planes):
-    depth = arrived.shape[0] // runs
-    width = depth // SLOTS
+def collate_kernel(arrived, out, *, planes, width):
+    beside = CORES * SIDE
+    depth = arrived.shape[0] // beside
+    runs = planes * beside
     piece = out.shape[0] // planes
     tile = (piece - 2) // width
     group = LANES // SLOTS
     step = 32.0
+    tags = [jnp.zeros((1, LANES), jnp.float32) for _ in range(runs // group)]
+    for q in range(beside):
+        lines = arrived[(q + 1) * depth - SLOTS : (q + 1) * depth, :].astype(jnp.float32)
+        first = q * planes // group
+        for g in range(first, ((q + 1) * planes - 1) // group + 1):
+            tags[g] = tags[g] + lines[g - first : g - first + 1]
     codes = []
     for g in range(runs // group):
-        tag = jnp.zeros((2, LANES), jnp.float32)
-        for r in range(g * group, (g + 1) * group):
-            at = r * depth + width * SLOTS
-            tag = tag + arrived[at : at + 2, :].astype(jnp.float32)
         run = lax.shift_right_logical(lax.broadcasted_iota(jnp.int32, (1, LANES), 1), 4) + g * group
         plane = run
         for wrap in range(planes, runs, planes):
             plane = plane - jnp.where(run >= wrap, planes, 0)
-        codes.append(jnp.where(tag[:1] > 0.0, tag[:1] + step * plane.astype(jnp.float32), 0.0))
+        codes.append(jnp.where(tags[g] > 0.0, tags[g] + step * plane.astype(jnp.float32), 0.0))
     codes = jnp.concatenate(codes, axis=1)
     site = lax.broadcasted_iota(jnp.int32, (tile, codes.shape[1]), 0).astype(jnp.float32) + 1.0
     pickers = [jnp.where(codes == site + step * z, 1.0, 0.0) for z in range(planes)]
@@ -172,28 +194,30 @@
     for r in range(runs):
         parts = []
         for part in range(width):
-            at = r * depth + part * SLOTS
+            at = r // planes * depth + (r % planes * width + part) * SLOTS
             parts.append(arrived[at : at + SLOTS, :])
         rows.append(jnp.concatenate(parts, axis=1))
     rows = jnp.concatenate(rows, axis=0)
     sums = jnp.dot(picker, rows, preferred_element_type=jnp.float32)
+    order = plane_order(planes)
     for z in range(planes):
         powers = []
+        first = order.index(z) * piece
         for part in range(width):
             coded, power = encoded(
                 sums[z * tile : (z + 1) * tile, part * LANES : (part + 1) * LANES]
             )
-            at = z * piece + part * tile
+            at = first + part * tile
             out[at : at + tile, :] = coded
             powers.append(power)
         powers = jnp.concatenate(powers, axis=0).astype(jnp.int32).astype(jnp.int16)
-        at = z * piece + width * tile
+        at = first + width * tile
         out[at : at + width, :] = powers
 
 
-def collate(arrived, runs, planes, tile, cols):
-    return pl.pallas_call(
-        functools.partial(collate_kernel, runs=runs, planes=planes),
+def collate(arrived, planes, tile, cols):
+    return pl.pallas_call(
+        functools.partial(collate_kernel, planes=planes, width=cols // LANES),
         in_specs=[pl.BlockSpec(memory_space=pltpu.VMEM)],
         out_specs=pl.BlockSpec(memory_space=pltpu.VMEM),
         out_shape=pltpu.VMEM((planes * (cols // LANES * tile + 2), LANES), jnp.int16),
@@ -238,8 +262,8 @@
     dpiece = LANES // 2
     bwidth = width * 2
     low = lax.broadcasted_iota(jnp.int32, (tile, LANES), 1) < dpiece
-    for two in range(count // 2):
-        span = slice(two * LANES, (two + 1) * LANES)
+    for two, place in enumerate(part_order(count // 2)):
+        span = slice(place * LANES, (place + 1) * LANES)
         both = []
         for j in (2 * two, 2 * two + 1):
             both += decoded(pieces, j * piece, tile, width)
@@ -247,6 +271,7 @@
             a, b = both[half], both[width + half]
             sums[2 * half, :, span] = jnp.where(low, a, pltpu.roll(b, dpiece, 1))
             sums[2 * half + 1, :, span] = jnp.where(low, pltpu.roll(a, dpiece, 1), b)
+    order = last_order(pairs * bwidth)
     some = 6
     for first in range(0, pairs, some):
         totals = [[jnp.zeros((8, LANES), jnp.float32) for _ in range(bwidth)] for _ in range(some)]
@@ -259,7 +284,7 @@
                         totals[i][b] = totals[i][b] + t * s[b]
         for i in range(some):
             for b in range(bwidth):
-                at = (first + i) * bwidth + b
+                at = order.index((first + i) * bwidth + b)
                 ends[at : at + 1, :] = jnp.sum(totals[i][b], axis=0, keepdims=True)
     total = jnp.sum(ends[...], axis=1, keepdims=True)
     out[...] = jnp.broadcast_to(total, ends.shape)[:, None, :]
@@ -281,6 +306,20 @@
         pltpu.with_memory_space_constraint(amplitudes, pltpu.VMEM),
         pltpu.with_memory_space_constraint(pieces, pltpu.VMEM),
     )
+
+
+def finish_kernel(shares, out):
+    out[...] = jnp.sum(shares[:, 0, :], axis=0, keepdims=True)
+
+
+def finish(shares):
+    return pl.pallas_call(
+        finish_kernel,
+        in_specs=[pl.BlockSpec(memory_space=pltpu.VMEM)],
+        out_specs=pl.BlockSpec(memory_space=pltpu.VMEM),
+        out_shape=pltpu.VMEM((1, shares.shape[2]), jnp.float32),
+        name="finish",
+    )(pltpu.with_memory_space_constraint(shares, pltpu.VMEM))
 
 
 def exchanged(rows, axis, groups=None):
@@ -305,20 +344,29 @@
         for s in range(SIDE)
     ]
     beside = [[at[s][z][c] for s in range(SIDE) for c in range(CORES)] for z in range(planes)]
-    along = [[at[s][z][c] for z in range(planes)] for s in range(SIDE) for c in range(CORES)]
+    order = plane_order(planes)
+    along = [[at[s][z][c] for z in order] for s in range(SIDE) for c in range(CORES)]
+    across = [[2 * pair + half for pair in part_order(parts // 2) for half in range(2)]]
     place = lax.axis_index("cd").astype(jnp.int32).reshape(1)
     right = jnp.transpose(right_factor, (1, 2, 0)).reshape(cols, naux)
     message = form(
         heights, place, owner_map.reshape(1, rows), row_site, left_factor, right, formers
     )
     arrived = exchanged(message, "cd", beside)
-    collated = collate(arrived, formers, planes, tile, cols)
+    collated = collate(arrived, planes, tile, cols)
     planar = exchanged(collated, "cd", along)
     coded = combine(planar, planes, parts, tile, cols)
-    pieces = exchanged(coded, "ij")
+    pieces = exchanged(coded, "ij", across)
     partial = contract(amplitudes, pieces, parts, bwidth)
-    shares = lax.all_to_all(partial, "cd", split_axis=0, concat_axis=0, tiled=True)
-    return shares[:, 0, 0].sum(axis=0, keepdims=True)
+    shares = lax.all_to_all(
+        partial,
+        "cd",
+        split_axis=0,
+        concat_axis=0,
+        tiled=True,
+        axis_index_groups=[last_order(formers)],
+    )
+    return finish(shares)[0, :1]
 
 
 def solution(mesh):

time: 82 us -> 74.3 us (0.906)
  blocking collectives: 74.7 us -> 67 us
    all_to_all x3, blocking collectives: 57.4 us -> 50.1 us  [exchanged(): lax.all_to_all(tiles, axis, split_axis=0, concat_axis=0, tiled=True, axis...]
where the time goes in v4:
time: 74.3 us; the launch traced here: 74 us
  blocking collectives  67 us (90%)
  Pallas kernels  5.76 us (8%)
    all_to_all x3, blocking collectives, exchanged(): lax.all_to_all(tiles, axis, split_axis=0, concat_axis=0, tiled=True, axis...  50.1 us
    all_to_all x1, blocking collectives, on_device(): lax.all_to_all(partial, 'cd', split_axis=0, concat_axis=0, tiled=True, ax...  17 us
    pallas_call x1, Pallas kernels, form(): pl.pallas_call(form_kernel, in_specs=[pl.BlockSpec(memory_space=pltpu.SME...  4.66 us

profile of v4, /device:TPU:1, one launch (start us, length us, event | category | flops | bytes accessed | tf_op | source)
XLA Modules:
  0.0 74.0 jit_solution(1031929094511140949)
XLA Ops:
  0.7 4.7 %form.1 = bf16[1600,128]{1,0:T(8,128)(2,1)S(1)} custom-call(s32[1]{0:T(128)S(6)} %copy.7.heights, s32[1]{0:T(128)} %bitcast.place, s32[1,512]{1,0:T(1,128)} %bitcast.21, s32[1,512]{1,0:T(1,128)} %sites_hbm.1, bf16[512,4096]{1,0:T(8,128)(2,1)} %left_hbm.1, bf16[256,4096]{1,0:T(8,128)(2,1)} %bitcast.20), custom_call_target="tpu_custom_call" | custom-call | tf_op jit(solution)/shard_map/form/pallas_call | solution.py:126
  5.3 0.0 copy-start
  5.3 20.1 %all_to_all.20 = bf16[4,200,2,128]{3,2,1,0:T(2,128)(2,1)S(1)} all-to-all(bf16[4,200,2,128]{3,2,1,0:T(2,128)(2,1)S(1)} %bitcast.13), channel_id=1, replica_groups={{0,16,384,400},{32,48,416,432},{64,80,448,464},{96,112,480,496},{128,14..., dimensions={0} | all-to-all | bytes 819200 | tf_op jit(solution)/shard_map/all_to_all | solution.py:328
  25.4 0.4 collate.1
  25.8 14.9 %all_to_all.21 = s16[12,25,2,128]{3,2,1,0:T(2,128)(2,1)S(1)} all-to-all(s16[12,25,2,128]{3,2,1,0:T(2,128)(2,1)S(1)} %bitcast.17), channel_id=1, replica_groups={{288,96,320,128,352,160,0,192,32,224,64,256},{304,112,336,144,368,176,1..., dimensions={0} | all-to-all | bytes 307200 | tf_op jit(solution)/shard_map/all_to_all | solution.py:328
  40.6 0.1 combine.1
  40.8 15.1 %all_to_all.22 = s16[16,25,2,128]{3,2,1,0:T(2,128)(2,1)S(1)} all-to-all(s16[16,25,2,128]{3,2,1,0:T(2,128)(2,1)S(1)} %bitcast.15), channel_id=1, replica_groups={{8,9,2,3,12,13,6,7,0,1,10,11,4,5,14,15},{24,25,18,19,28,29,22,23,16,17,..., dimensions={0} | all-to-all | bytes 409600 | tf_op jit(solution)/shard_map/all_to_all | solution.py:328
  55.9 0.0 copy-done
  55.9 0.6 contract.1
  56.5 17.0 %all_to_all.23.shares = f32[48,1,128]{2,1,0:T(1,128)S(1)} all-to-all(f32[48,1,128]{2,1,0:T(1,128)S(1)} %contract.1), channel_id=1, replica_groups={{256,272,288,304,320,336,352,368,384,400,416,432,448,464,480,496,512,52..., dimensions={0} | all-to-all | bytes 49152 | tf_op jit(solution)/shard_map/all_to_all | solution.py:361
  73.5 0.0 copy-start.1
  73.5 0.5 copy-done.1
  (1 shorter events, 0.0 us)
Async XLA Ops:
  5.3 50.6 %copy-start = (f32[12,24,1024]{2,1,0:T(8,128)S(1)}, f32[12,24,1024]{2,1,0:T(8,128)}, u32[]{:S(2)}) copy-start(f32[12,24,1024]{2,1,0:T(8,128)} %amplitudes.1) | copy-start | bytes 3538948
  73.5 0.5 copy-start.1

commit v5 on v4

--- a/solution.py
+++ b/solution.py
@@ -265,7 +265,7 @@
     for two, place in enumerate(part_order(count // 2)):
         span = slice(place * LANES, (place + 1) * LANES)
         both = []
-        for j in (2 * two, 2 * two + 1):
+        for j in (2 * two + 1, 2 * two):
             both += decoded(pieces, j * piece, tile, width)
         for half in range(width):
             a, b = both[half], both[width + half]
@@ -346,7 +346,7 @@
     beside = [[at[s][z][c] for s in range(SIDE) for c in range(CORES)] for z in range(planes)]
     order = plane_order(planes)
     along = [[at[s][z][c] for z in order] for s in range(SIDE) for c in range(CORES)]
-    across = [[2 * pair + half for pair in part_order(parts // 2) for half in range(2)]]
+    across = [[2 * pair + half for pair in part_order(parts // 2) for half in (1, 0)]]
     place = lax.axis_index("cd").astype(jnp.int32).reshape(1)
     right = jnp.transpose(right_factor, (1, 2, 0)).reshape(cols, naux)
     message = form(

time: 74.3 us -> 72.4 us (0.974)
  blocking collectives: 67 us -> 65.2 us
    all_to_all x3, blocking collectives: 50.1 us -> 49.1 us  [exchanged(): lax.all_to_all(tiles, axis, split_axis=0, concat_axis=0, tiled=True, axis...]
    all_to_all x1, blocking collectives: 17 us -> 16.1 us  [on_device(): lax.all_to_all(partial, 'cd', split_axis=0, concat_axis=0, tiled=True, ax...]
where the time goes in v5:
time: 72.4 us; the launch traced here: 72.2 us
  blocking collectives  65.2 us (90%)
  Pallas kernels  5.77 us (8%)
    all_to_all x3, blocking collectives, exchanged(): lax.all_to_all(tiles, axis, split_axis=0, concat_axis=0, tiled=True, axis...  49.1 us
    all_to_all x1, blocking collectives, on_device(): lax.all_to_all(partial, 'cd', split_axis=0, concat_axis=0, tiled=True, ax...  16.1 us
    pallas_call x1, Pallas kernels, form(): pl.pallas_call(form_kernel, in_specs=[pl.BlockSpec(memory_space=pltpu.SME...  4.66 us

profile of v5, /device:TPU:1, one launch (start us, length us, event | category | flops | bytes accessed | tf_op | source)
XLA Modules:
  0.0 72.2 jit_solution(10267895550289389482)
XLA Ops:
  0.7 4.7 %form.1 = bf16[1600,128]{1,0:T(8,128)(2,1)S(1)} custom-call(s32[1]{0:T(128)S(6)} %copy.7.heights, s32[1]{0:T(128)} %bitcast.place, s32[1,512]{1,0:T(1,128)} %bitcast.21, s32[1,512]{1,0:T(1,128)} %sites_hbm.1, bf16[512,4096]{1,0:T(8,128)(2,1)} %left_hbm.1, bf16[256,4096]{1,0:T(8,128)(2,1)} %bitcast.20), custom_call_target="tpu_custom_call" | custom-call | tf_op jit(solution)/shard_map/form/pallas_call | solution.py:126
  5.3 0.0 copy-start
  5.3 20.1 %all_to_all.20 = bf16[4,200,2,128]{3,2,1,0:T(2,128)(2,1)S(1)} all-to-all(bf16[4,200,2,128]{3,2,1,0:T(2,128)(2,1)S(1)} %bitcast.13), channel_id=1, replica_groups={{0,16,384,400},{32,48,416,432},{64,80,448,464},{96,112,480,496},{128,14..., dimensions={0} | all-to-all | bytes 819200 | tf_op jit(solution)/shard_map/all_to_all | solution.py:328
  25.4 0.4 collate.1
  25.8 14.9 %all_to_all.21 = s16[12,25,2,128]{3,2,1,0:T(2,128)(2,1)S(1)} all-to-all(s16[12,25,2,128]{3,2,1,0:T(2,128)(2,1)S(1)} %bitcast.17), channel_id=1, replica_groups={{288,96,320,128,352,160,0,192,32,224,64,256},{304,112,336,144,368,176,1..., dimensions={0} | all-to-all | bytes 307200 | tf_op jit(solution)/shard_map/all_to_all | solution.py:328
  40.6 0.1 combine.1
  40.8 14.2 %all_to_all.22 = s16[16,25,2,128]{3,2,1,0:T(2,128)(2,1)S(1)} all-to-all(s16[16,25,2,128]{3,2,1,0:T(2,128)(2,1)S(1)} %bitcast.15), channel_id=1, replica_groups={{9,8,3,2,13,12,7,6,1,0,11,10,5,4,15,14},{25,24,19,18,29,28,23,22,17,16,..., dimensions={0} | all-to-all | bytes 409600 | tf_op jit(solution)/shard_map/all_to_all | solution.py:328
  55.0 0.0 copy-done
  55.0 0.6 contract.1
  55.5 16.1 %all_to_all.23.shares = f32[48,1,128]{2,1,0:T(1,128)S(1)} all-to-all(f32[48,1,128]{2,1,0:T(1,128)S(1)} %contract.1), channel_id=1, replica_groups={{256,272,288,304,320,336,352,368,384,400,416,432,448,464,480,496,512,52..., dimensions={0} | all-to-all | bytes 49152 | tf_op jit(solution)/shard_map/all_to_all | solution.py:361
  71.7 0.0 copy-start.1
  71.7 0.5 copy-done.1
  (1 shorter events, 0.0 us)
Async XLA Ops:
  5.3 49.6 %copy-start = (f32[12,24,1024]{2,1,0:T(8,128)S(1)}, f32[12,24,1024]{2,1,0:T(8,128)}, u32[]{:S(2)}) copy-start(f32[12,24,1024]{2,1,0:T(8,128)} %amplitudes.1) | copy-start | bytes 3538948
  71.7 0.5 copy-start.1
